TPU v7x, 32 devices: a whole 2x2x4 slice. The times are simulated.
32 devices in a mesh: elem: 16 (over z, x, core), band: 2 (over y).
Axes of the slice: x: 2, y: 2, z: 4, core: 2. Of those that a mesh axis runs over, the one named last changes fastest.
Arguments:
- basis: bfloat16 [256, 32, 16, 160], P('band', 'elem'), may hold values from -8 to 8
- hamiltonian: bfloat16 [32, 16, 7, 160, 160], P('elem'), may hold values from -0.09375 to 0.09375
- neighbours: int32 [32, 16, 6], P('elem'), may hold values from 0 to 511, as said below
Outputs:
- filtered: bfloat16 [256, 32, 16, 160], P('band', 'elem')
- intersection: float32 [256, 256], P('elem', 'band')
- projected: float32 [256, 256], P('elem', 'band')
Inputs may be any that keep to these rules, and one draw needn't show every extreme that they name: neighbours[z, s, d] = z2 * 16 + s2 names the element (z2, s2) that shares face d with element (z, s) on a periodic grid of 4 x 4 x 32 cells, whose cells are stored within each layer in an order of the draw; faces 0 to 3 lie in the same layer z, face 4 in layer z - 1 and face 5 in layer z + 1, both modulo 32.
All inputs are finite; a program needn't handle non-finite values.
Results may differ from a plain program's by a relative error of at most 0.0075.
Values may be sent and summed in bfloat16 or wider, within the bound.
A program may use at most 64 MiB of HBM per device.

v0:
```python
import jax
import jax.numpy as jnp
from jax import lax
from jax.sharding import PartitionSpec as P

DEGREE = 4


def extended_2(block, sides, width):
    for axis, dim in sides:
        count = lax.axis_size(axis)
        forward = [(i, i + 1) for i in range(count - 1)]
        forward.append((count - 1, 0))
        backward = [(target, source) for source, target in forward]
        low = lax.ppermute(
            lax.slice_in_dim(block, block.shape[dim] - width, None, axis=dim), axis, forward
        )
        high = lax.ppermute(lax.slice_in_dim(block, 0, width, axis=dim), axis, backward)
        block = jnp.concatenate([low, block, high], axis=dim)
    return block


def body(basis, hamiltonian, neighbours):
    width, layers, cells, functions = basis.shape
    elem_count = lax.axis_size("elem")
    depth = layers * elem_count
    first = lax.axis_index("elem") * layers
    layer_of = neighbours // cells
    relative = (layer_of - first + 1) % depth
    outer = relative * cells + neighbours % cells
    own = (jnp.arange(layers)[:, None] + 1) * cells + jnp.arange(cells)[None, :]
    table = jnp.concatenate([own[:, :, None], outer], axis=2)

    def apply_blocks(field):
        extended = extended_2(field, (("elem", 1),), 1)
        flat = extended.reshape(width, (layers + 2) * cells, functions)
        picked = jnp.take(flat, table, axis=1)
        return jnp.einsum(
            "zsdij,czsdj->czsi", hamiltonian, picked, preferred_element_type=jnp.float32
        )

    previous = basis
    current = apply_blocks(basis).astype(jnp.bfloat16)
    for step in range(DEGREE - 1):
        following = (2.0 * apply_blocks(current) - previous.astype(jnp.float32)).astype(
            jnp.bfloat16
        )
        previous, current = (current, following)
    image = apply_blocks(current).astype(jnp.bfloat16)
    factor = 1.0 / (depth * cells * functions)
    piece = lax.all_gather(current, "band", axis=0, tiled=True)
    left_part = jnp.einsum("kzsi,czsi->kc", piece, current, preferred_element_type=jnp.float32)
    right_part = jnp.einsum("kzsi,czsi->kc", piece, image, preferred_element_type=jnp.float32)
    partial_terms = jnp.stack([left_part, right_part])
    totals = lax.psum_scatter(partial_terms, "elem", scatter_dimension=1, tiled=True)
    return (current, totals[0] * factor, totals[1] * factor)


def solution(mesh):
    placed = (
        P("band", "elem", None, None),
        P("elem", None, None, None, None),
        P("elem", None, None),
    )
    return jax.shard_map(
        body,
        mesh=mesh,
        in_specs=placed,
        out_specs=(P("band", "elem", None, None), P("elem", "band"), P("elem", "band")),
        check_vma=False,
    )
```

profile of v0, /device:TPU:0, one launch (start us, length us, event | category | flops | bytes accessed | tf_op | source)
XLA Modules:
  0.0 281.0 jit_solution(16922853320731717165)
XLA Ops:
  8.6 5.5 %collective-permute-start.1 = (bf16[128,1,16,160]{0,3,2,1:T(8,128)(2,1)S(1)}, bf16[128,1,16,160]{0,3,2,1:T(8,128)(2,1)S(1)}, u32[]{:S(2)}, u32[]{:S(2)}) collective-permute-start(bf16[128,1,16,160]{0,3,2,1:T(8,128)(2,1)S(1)} %get-tuple-element.15), channel_id=1, source_target_pairs={{2,0},{4,2},{6,4},{8,6},{10,8},{12,10},{14,12},{16,14},{18,16},{20... | collective-permute-start | bytes 1966088 | tf_op jit(solution)/shard_map/ppermute | solution.py:18
  14.6 7.6 %collective-permute-done.1 = bf16[128,1,16,160]{0,3,2,1:T(8,128)(2,1)S(1)} collective-permute-done((bf16[128,1,16,160]{0,3,2,1:T(8,128)(2,1)S(1)}, bf16[128,1,16,160]{0,3,2,1:T(8,128)(2,1)S(1)}, u32[]{:S(2)}, u32[]{:S(2)}) %collective-permute-start.1) | collective-permute-done | bytes 655392 | tf_op jit(solution)/shard_map/ppermute | solution.py:18
  22.2 4.8 %collective-permute-done = bf16[128,1,16,160]{0,3,2,1:T(8,128)(2,1)} collective-permute-done((bf16[128,1,16,160]{0,3,2,1:T(8,128)(2,1)S(1)}, bf16[128,1,16,160]{0,3,2,1:T(8,128)(2,1)}, u32[]{:S(2)}, u32[]{:S(2)}) %collective-permute-start) | collective-permute-done | bytes 655392 | tf_op jit(solution)/shard_map/ppermute | solution.py:15
  28.8 9.4 %gather_fusion = bf16[224,128,160]{1,2,0:T(8,128)(2,1)} fusion(bf16[128,64,160]{0,2,1:T(8,128)(2,1)S(1)} %bitcast.108, s32[1024]{0:T(1024)S(1)} %pad_clamp_fusion), kind=kCustom, calls=%fused_computation.clone | custom fusion | bytes 18350976 | tf_op jit(solution)/shard_map/jit(_take)/gather | solution.py:37
  38.2 11.3 %fusion.42 = bf16[128,2,16,160]{0,3,2,1:T(8,128)(2,1)S(1)} fusion(bf16[2,16,7,160,160]{4,3,2,1,0:T(8,128)(2,1)} %param.6, bf16[2,16,7,128,160]{3,4,2,1,0:T(8,128)(2,1)} %bitcast.114, pred[2,16,7]{2,1,0:T(8,128)(4,1)S(1)} %copy.14), kind=kOutput, calls=%fused_computation.49 | convolution fusion | flops 1473249280 | bytes 21954784 | tf_op jit(solution)/shard_map/zsdij,czsdj->czsi/dot_general | solution.py:38
  50.2 7.6 %collective-permute-done.3 = bf16[128,1,16,160]{0,3,2,1:T(8,128)(2,1)S(1)} collective-permute-done((bf16[128,1,16,160]{0,3,2,1:T(8,128)(2,1)S(1)}, bf16[128,1,16,160]{0,3,2,1:T(8,128)(2,1)S(1)}, u32[]{:S(2)}, u32[]{:S(2)}) %collective-permute-start.3) | collective-permute-done | bytes 655392 | tf_op jit(solution)/shard_map/ppermute | solution.py:18
  57.8 5.2 %collective-permute-done.2 = bf16[128,1,16,160]{0,3,2,1:T(8,128)(2,1)S(1)} collective-permute-done((bf16[128,1,16,160]{0,3,2,1:T(8,128)(2,1)S(1)}, bf16[128,1,16,160]{0,3,2,1:T(8,128)(2,1)S(1)}, u32[]{:S(2)}, u32[]{:S(2)}) %collective-permute-start.2) | collective-permute-done | bytes 655392 | tf_op jit(solution)/shard_map/ppermute | solution.py:15
  63.3 9.4 %gather_fusion.1 = bf16[224,128,160]{1,2,0:T(8,128)(2,1)} fusion(bf16[128,64,160]{0,2,1:T(8,128)(2,1)S(1)} %bitcast.109, s32[1024]{0:T(1024)S(1)} %pad_clamp_fusion), kind=kCustom, calls=%fused_computation.1.clone | custom fusion | bytes 18350976 | tf_op jit(solution)/shard_map/jit(_take)/gather | solution.py:37
  72.7 11.8 %fusion.25 = bf16[128,2,16,160]{0,3,2,1:T(8,128)(2,1)S(1)} fusion(bf16[128,2,16,160]{0,3,2,1:T(8,128)(2,1)} %param.5, bf16[2,16,7,160,160]{4,3,2,1,0:T(8,128)(2,1)} %param.6, bf16[2,16,7,128,160]{3,4,2,1,0:T(8,128)(2,1)} %bitcast.115, pred[2,16,7]{2,1,0:T(8,128)(4,1)S(1)} %copy.14), kind=kOutput, calls=%fused_computation.42 | convolution fusion | flops 1475215360 | bytes 23265504 | tf_op jit(solution)/shard_map/zsdij,czsdj->czsi/dot_general | solution.py:38
  84.7 4.0 %collective-permute-start.4 = (bf16[128,1,16,160]{0,3,2,1:T(8,128)(2,1)S(1)}, bf16[128,1,16,160]{0,3,2,1:T(8,128)(2,1)S(1)}, u32[]{:S(2)}, u32[]{:S(2)}) collective-permute-start(bf16[128,1,16,160]{0,3,2,1:T(8,128)(2,1)S(1)} %get-tuple-element.10), channel_id=1, source_target_pairs={{0,2},{2,4},{4,6},{6,8},{8,10},{10,12},{12,14},{14,16},{16,18},{18... | collective-permute-start | bytes 1966088 | tf_op jit(solution)/shard_map/ppermute | solution.py:15
  88.7 4.1 %collective-permute-done.5 = bf16[128,1,16,160]{0,3,2,1:T(8,128)(2,1)S(1)} collective-permute-done((bf16[128,1,16,160]{0,3,2,1:T(8,128)(2,1)S(1)}, bf16[128,1,16,160]{0,3,2,1:T(8,128)(2,1)S(1)}, u32[]{:S(2)}, u32[]{:S(2)}) %collective-permute-start.5) | collective-permute-done | bytes 655392 | tf_op jit(solution)/shard_map/ppermute | solution.py:18
  92.8 7.4 %collective-permute-done.4 = bf16[128,1,16,160]{0,3,2,1:T(8,128)(2,1)S(1)} collective-permute-done((bf16[128,1,16,160]{0,3,2,1:T(8,128)(2,1)S(1)}, bf16[128,1,16,160]{0,3,2,1:T(8,128)(2,1)S(1)}, u32[]{:S(2)}, u32[]{:S(2)}) %collective-permute-start.4) | collective-permute-done | bytes 655392 | tf_op jit(solution)/shard_map/ppermute | solution.py:15
  100.5 9.4 %gather_fusion.2 = bf16[224,128,160]{1,2,0:T(8,128)(2,1)} fusion(bf16[128,64,160]{0,2,1:T(8,128)(2,1)S(1)} %bitcast.110, s32[1024]{0:T(1024)S(1)} %pad_clamp_fusion), kind=kCustom, calls=%fused_computation.2.clone | custom fusion | bytes 18350976 | tf_op jit(solution)/shard_map/jit(_take)/gather | solution.py:37
  109.9 11.8 %fusion.24 = bf16[128,2,16,160]{0,3,2,1:T(8,128)(2,1)S(1)} fusion(bf16[128,2,16,160]{0,3,2,1:T(8,128)(2,1)} %copy-done.2, bf16[2,16,7,160,160]{4,3,2,1,0:T(8,128)(2,1)} %param.6, bf16[2,16,7,128,160]{3,4,2,1,0:T(8,128)(2,1)} %bitcast.112, pred[2,16,7]{2,1,0:T(8,128)(4,1)S(1)} %copy.14), kind=kOutput, calls=%fused_computation.39 | convolution fusion | flops 1475215360 | bytes 23265504 | tf_op jit(solution)/shard_map/zsdij,czsdj->czsi/dot_general | solution.py:38
  121.8 5.8 %collective-permute-start.6 = (bf16[128,1,16,160]{0,3,2,1:T(8,128)(2,1)S(1)}, bf16[128,1,16,160]{0,3,2,1:T(8,128)(2,1)S(1)}, u32[]{:S(2)}, u32[]{:S(2)}) collective-permute-start(bf16[128,1,16,160]{0,3,2,1:T(8,128)(2,1)S(1)} %get-tuple-element.8), channel_id=1, source_target_pairs={{0,2},{2,4},{4,6},{6,8},{8,10},{10,12},{12,14},{14,16},{16,18},{18... | collective-permute-start | bytes 1966088 | tf_op jit(solution)/shard_map/ppermute | solution.py:15
  129.9 6.1 %collective-permute-done.6 = bf16[128,1,16,160]{0,3,2,1:T(8,128)(2,1)S(1)} collective-permute-done((bf16[128,1,16,160]{0,3,2,1:T(8,128)(2,1)S(1)}, bf16[128,1,16,160]{0,3,2,1:T(8,128)(2,1)S(1)}, u32[]{:S(2)}, u32[]{:S(2)}) %collective-permute-start.6) | collective-permute-done | bytes 655392 | tf_op jit(solution)/shard_map/ppermute | solution.py:15
  136.3 9.4 %gather_fusion.3 = bf16[224,128,160]{1,2,0:T(8,128)(2,1)} fusion(bf16[128,64,160]{0,2,1:T(8,128)(2,1)S(1)} %bitcast.106, s32[1024]{0:T(1024)S(1)} %pad_clamp_fusion), kind=kCustom, calls=%fused_computation.3.clone | custom fusion | bytes 18350976 | tf_op jit(solution)/shard_map/jit(_take)/gather | solution.py:37
  145.7 12.9 %fusion.23 = bf16[128,2,16,160]{0,3,2,1:T(8,128)(2,1)} fusion(bf16[128,2,16,160]{0,3,2,1:T(8,128)(2,1)} %copy-done.1, bf16[2,16,7,160,160]{4,3,2,1,0:T(8,128)(2,1)} %param.6, bf16[2,16,7,128,160]{3,4,2,1,0:T(8,128)(2,1)} %bitcast.113, pred[2,16,7]{2,1,0:T(8,128)(4,1)S(1)} %copy.14), kind=kOutput, calls=%fused_computation.36 | convolution fusion | flops 1475215360 | bytes 23265504 | tf_op jit(solution)/shard_map/zsdij,czsdj->czsi/dot_general | solution.py:38
  160.2 6.8 %collective-permute-start.8 = (bf16[128,1,16,160]{0,3,2,1:T(8,128)(2,1)S(1)}, bf16[128,1,16,160]{0,3,2,1:T(8,128)(2,1)S(1)}, u32[]{:S(2)}, u32[]{:S(2)}) collective-permute-start(bf16[128,1,16,160]{0,3,2,1:T(8,128)(2,1)S(1)} %get-tuple-element.6), channel_id=1, source_target_pairs={{0,2},{2,4},{4,6},{6,8},{8,10},{10,12},{12,14},{14,16},{16,18},{18... | collective-permute-start | bytes 1966088 | tf_op jit(solution)/shard_map/ppermute | solution.py:15
  168.6 6.5 %collective-permute-done.8 = bf16[128,1,16,160]{0,3,2,1:T(8,128)(2,1)S(1)} collective-permute-done((bf16[128,1,16,160]{0,3,2,1:T(8,128)(2,1)S(1)}, bf16[128,1,16,160]{0,3,2,1:T(8,128)(2,1)S(1)}, u32[]{:S(2)}, u32[]{:S(2)}) %collective-permute-start.8) | collective-permute-done | bytes 655392 | tf_op jit(solution)/shard_map/ppermute | solution.py:15
  175.4 9.4 %gather_fusion.4 = bf16[224,128,160]{1,2,0:T(8,128)(2,1)} fusion(bf16[128,64,160]{0,2,1:T(8,128)(2,1)S(1)} %bitcast.107, s32[1024]{0:T(1024)S(1)} %pad_clamp_fusion), kind=kCustom, calls=%fused_computation.4.clone | custom fusion | bytes 18350976 | tf_op jit(solution)/shard_map/jit(_take)/gather | solution.py:37
  184.8 17.0 %all-gather.2.cloned.1.call-done = bf16[256,2,16,160]{0,3,2,1:T(8,128)(2,1)} async-done(((bf16[128,2,16,160]{0,3,2,1:T(8,128)(2,1)}), bf16[256,2,16,160]{0,3,2,1:T(8,128)(2,1)}) %all-gather.2.cloned.1.call-update) | async-done | bytes 2621456 | tf_op jit(solution)/shard_map/all_gather | solution.py:51
  205.0 11.3 %fusion.60 = f32[1,256,128]{2,1,0:T(8,128)S(1)} fusion(bf16[2,16,7,160,160]{4,3,2,1,0:T(8,128)(2,1)} %param.6, bf16[256,2,16,160]{0,3,2,1:T(8,128)(2,1)S(1)} %copy-done.4, bf16[2,16,7,128,160]{3,4,2,1,0:T(8,128)(2,1)} %bitcast.111, pred[2,16,7]{2,1,0:T(8,128)(4,1)S(1)} %copy.14), kind=kOutput, calls=%fused_computation.53 | convolution fusion | flops 1808793600 | bytes 23396576 | tf_op jit(solution)/shard_map/kzsi,czsi->kc/dot_general | solution.py:53
  217.0 55.9 %reduce-scatter.2.cloned.1.call-done = f32[2,16,128]{2,1,0:T(8,128)} async-done(((f32[2,256,128]{2,1,0:T(8,128)}), f32[2,16,128]{2,1,0:T(8,128)}) %reduce-scatter.2.cloned.1.call-update) | async-done | bytes 16400 | tf_op jit(solution)/shard_map/reduce_scatter | solution.py:55
  (43 shorter events, 16.4 us)
Async XLA Ops:
  7.2 7.0 %copy-start.3 = (s32[2,16,6]{1,0,2:T(2,128)S(1)}, s32[2,16,6]{1,0,2:T(2,128)}, u32[]{:S(2)}) copy-start(s32[2,16,6]{1,0,2:T(2,128)} %param.7) | copy-start | bytes 2308
  7.2 194.6 %all-gather.2.cloned.1.call-start = ((), (), s32[]{:S(2)}) async-start(), calls=%async_computation.1 | async-start | bytes 3932160 | tf_op jit(solution)/shard_map/all_gather | solution.py:51
  8.6 13.6 %collective-permute-start.1 = (bf16[128,1,16,160]{0,3,2,1:T(8,128)(2,1)S(1)}, bf16[128,1,16,160]{0,3,2,1:T(8,128)(2,1)S(1)}, u32[]{:S(2)}, u32[]{:S(2)}) collective-permute-start(bf16[128,1,16,160]{0,3,2,1:T(8,128)(2,1)S(1)} %get-tuple-element.15), channel_id=1, source_target_pairs={{2,0},{4,2},{6,4},{8,6},{10,8},{12,10},{14,12},{16,14},{18,16},{20... | collective-permute-start | bytes 1966088 | tf_op jit(solution)/shard_map/ppermute | solution.py:18
  14.1 12.9 %collective-permute-start = (bf16[128,1,16,160]{0,3,2,1:T(8,128)(2,1)S(1)}, bf16[128,1,16,160]{0,3,2,1:T(8,128)(2,1)}, u32[]{:S(2)}, u32[]{:S(2)}) collective-permute-start(bf16[128,1,16,160]{0,3,2,1:T(8,128)(2,1)S(1)} %get-tuple-element.14), channel_id=1, source_target_pairs={{0,2},{2,4},{4,6},{6,8},{8,10},{10,12},{12,14},{14,16},{16,18},{18... | collective-permute-start | bytes 1966088 | tf_op jit(solution)/shard_map/ppermute | solution.py:15
  49.5 13.8 %copy-start.2 = (bf16[128,2,16,160]{0,3,2,1:T(8,128)(2,1)}, bf16[128,2,16,160]{0,3,2,1:T(8,128)(2,1)S(1)}, u32[]{:S(2)}) copy-start(bf16[128,2,16,160]{0,3,2,1:T(8,128)(2,1)S(1)} %fusion.42) | copy-start | bytes 3932164
  49.6 8.2 %collective-permute-start.3 = (bf16[128,1,16,160]{0,3,2,1:T(8,128)(2,1)S(1)}, bf16[128,1,16,160]{0,3,2,1:T(8,128)(2,1)S(1)}, u32[]{:S(2)}, u32[]{:S(2)}) collective-permute-start(bf16[128,1,16,160]{0,3,2,1:T(8,128)(2,1)S(1)} %get-tuple-element.13), channel_id=1, source_target_pairs={{2,0},{4,2},{6,4},{8,6},{10,8},{12,10},{14,12},{16,14},{18,16},{20... | collective-permute-start | bytes 1966088 | tf_op jit(solution)/shard_map/ppermute | solution.py:18
  49.7 13.3 %collective-permute-start.2 = (bf16[128,1,16,160]{0,3,2,1:T(8,128)(2,1)S(1)}, bf16[128,1,16,160]{0,3,2,1:T(8,128)(2,1)S(1)}, u32[]{:S(2)}, u32[]{:S(2)}) collective-permute-start(bf16[128,1,16,160]{0,3,2,1:T(8,128)(2,1)S(1)} %get-tuple-element.12), channel_id=1, source_target_pairs={{0,2},{2,4},{4,6},{6,8},{8,10},{10,12},{12,14},{14,16},{16,18},{18... | collective-permute-start | bytes 1966088 | tf_op jit(solution)/shard_map/ppermute | solution.py:15
  84.5 15.9 %copy-start.1 = (bf16[128,2,16,160]{0,3,2,1:T(8,128)(2,1)}, bf16[128,2,16,160]{0,3,2,1:T(8,128)(2,1)S(1)}, u32[]{:S(2)}) copy-start(bf16[128,2,16,160]{0,3,2,1:T(8,128)(2,1)S(1)} %fusion.25) | copy-start | bytes 3932164
  84.6 8.2 %collective-permute-start.5 = (bf16[128,1,16,160]{0,3,2,1:T(8,128)(2,1)S(1)}, bf16[128,1,16,160]{0,3,2,1:T(8,128)(2,1)S(1)}, u32[]{:S(2)}, u32[]{:S(2)}) collective-permute-start(bf16[128,1,16,160]{0,3,2,1:T(8,128)(2,1)S(1)} %get-tuple-element.11), channel_id=1, source_target_pairs={{2,0},{4,2},{6,4},{8,6},{10,8},{12,10},{14,12},{16,14},{18,16},{20... | collective-permute-start | bytes 1966088 | tf_op jit(solution)/shard_map/ppermute | solution.py:18
  84.7 15.4 %collective-permute-start.4 = (bf16[128,1,16,160]{0,3,2,1:T(8,128)(2,1)S(1)}, bf16[128,1,16,160]{0,3,2,1:T(8,128)(2,1)S(1)}, u32[]{:S(2)}, u32[]{:S(2)}) collective-permute-start(bf16[128,1,16,160]{0,3,2,1:T(8,128)(2,1)S(1)} %get-tuple-element.10), channel_id=1, source_target_pairs={{0,2},{2,4},{4,6},{6,8},{8,10},{10,12},{12,14},{14,16},{16,18},{18... | collective-permute-start | bytes 1966088 | tf_op jit(solution)/shard_map/ppermute | solution.py:15
  121.8 8.2 %collective-permute-start.7 = (bf16[128,1,16,160]{0,3,2,1:T(8,128)(2,1)S(1)}, bf16[128,1,16,160]{0,3,2,1:T(8,128)(2,1)S(1)}, u32[]{:S(2)}, u32[]{:S(2)}) collective-permute-start(bf16[128,1,16,160]{0,3,2,1:T(8,128)(2,1)S(1)} %get-tuple-element.9), channel_id=1, source_target_pairs={{2,0},{4,2},{6,4},{8,6},{10,8},{12,10},{14,12},{16,14},{18,16},{20... | collective-permute-start | bytes 1966088 | tf_op jit(solution)/shard_map/ppermute | solution.py:18
  121.8 14.2 %collective-permute-start.6 = (bf16[128,1,16,160]{0,3,2,1:T(8,128)(2,1)S(1)}, bf16[128,1,16,160]{0,3,2,1:T(8,128)(2,1)S(1)}, u32[]{:S(2)}, u32[]{:S(2)}) collective-permute-start(bf16[128,1,16,160]{0,3,2,1:T(8,128)(2,1)S(1)} %get-tuple-element.8), channel_id=1, source_target_pairs={{0,2},{2,4},{4,6},{6,8},{8,10},{10,12},{12,14},{14,16},{16,18},{18... | collective-permute-start | bytes 1966088 | tf_op jit(solution)/shard_map/ppermute | solution.py:15
  158.6 114.3 %reduce-scatter.2.cloned.1.call-start = ((), (), s32[]{:S(2)}) async-start(), calls=%async_computation.2 | async-start | bytes 278528 | tf_op jit(solution)/shard_map/reduce_scatter | solution.py:55
  158.7 16.4 %copy-start = (bf16[128,2,16,160]{0,3,2,1:T(8,128)(2,1)S(1)}, bf16[128,2,16,160]{0,3,2,1:T(8,128)(2,1)}, u32[]{:S(2)}) copy-start(bf16[128,2,16,160]{0,3,2,1:T(8,128)(2,1)} %fusion.23) | copy-start | bytes 3932164
  160.2 8.4 %collective-permute-start.9 = (bf16[128,1,16,160]{0,3,2,1:T(8,128)(2,1)S(1)}, bf16[128,1,16,160]{0,3,2,1:T(8,128)(2,1)S(1)}, u32[]{:S(2)}, u32[]{:S(2)}) collective-permute-start(bf16[128,1,16,160]{0,3,2,1:T(8,128)(2,1)S(1)} %get-tuple-element.7), channel_id=1, source_target_pairs={{2,0},{4,2},{6,4},{8,6},{10,8},{12,10},{14,12},{16,14},{18,16},{20... | collective-permute-start | bytes 1966088 | tf_op jit(solution)/shard_map/ppermute | solution.py:18
  160.2 14.9 %collective-permute-start.8 = (bf16[128,1,16,160]{0,3,2,1:T(8,128)(2,1)S(1)}, bf16[128,1,16,160]{0,3,2,1:T(8,128)(2,1)S(1)}, u32[]{:S(2)}, u32[]{:S(2)}) collective-permute-start(bf16[128,1,16,160]{0,3,2,1:T(8,128)(2,1)S(1)} %get-tuple-element.6), channel_id=1, source_target_pairs={{0,2},{2,4},{4,6},{6,8},{8,10},{10,12},{12,14},{14,16},{16,18},{18... | collective-permute-start | bytes 1966088 | tf_op jit(solution)/shard_map/ppermute | solution.py:15
  201.8 3.1 %copy-start.4 = (bf16[256,2,16,160]{0,3,2,1:T(8,128)(2,1)S(1)}, bf16[256,2,16,160]{0,3,2,1:T(8,128)(2,1)}, u32[]{:S(2)}) copy-start(bf16[256,2,16,160]{0,3,2,1:T(8,128)(2,1)} %all-gather.2.cloned.1.call-done) | copy-start | bytes 7864324
Sparse Core Ops, SparseCore 0:
  158.7 43.0 all-gather.1
  217.1 55.7 reduce-scatter.1
where the time goes:
time: 281 us
  waiting for transfers between devices  126 us (45%)
  matrix products  62.2 us (22%)
  local copies, waits for them, and re-layouts  50.3 us (18%)
  starting transfers between devices  22.8 us (8%)
  between operations  14.2 us (5%)
  other arithmetic  5.15 us (2%)
    reduce_scatter x1, waiting for transfers between devices, body(): lax.psum_scatter(partial_terms, 'elem', scatter_dimension=1, tiled=True)  55.9 us
    dot_general x4, matrix products, apply_blocks(): jnp.einsum('zsdij,czsdj->czsi', hamiltonian, picked, preferred_element_ty...  47.8 us
    gather x5, local copies, waits for them, and re-layouts, apply_blocks(): picked = jnp.take(flat, table, axis=1)  46.9 us
    ppermute x5, waiting for transfers between devices, extended_2(): lax.ppermute(lax.slice_in_dim(block, block.shape[dim] - width, None, axis...  30 us
    ppermute x5, waiting for transfers between devices, extended_2(): lax.ppermute(lax.slice_in_dim(block, 0, width, axis=dim), axis, backward)  23.2 us
    ppermute x5, starting transfers between devices, extended_2(): lax.ppermute(lax.slice_in_dim(block, block.shape[dim] - width, None, axis...  17 us
    all_gather x1, waiting for transfers between devices, body(): piece = lax.all_gather(current, 'band', axis=0, tiled=True)  17 us
    dot_general x1, matrix products, body(): jnp.einsum('kzsi,czsi->kc', piece, image, preferred_element_type=jnp.floa...  11.3 us
  transfers between devices with their start and end apart: 12, of which 12 were waited for; matrix products, arithmetic and copies ran while one was open for 4% of the time, Pallas kernels for 0%

commit v1 on v0

--- a/solution.py
+++ b/solution.py
@@ -4,6 +4,18 @@
 from jax.sharding import PartitionSpec as P
 
 DEGREE = 4
+
+
+def gather_by_bits(x, axis, dim):
+    ways, here, step = (lax.axis_size(axis), lax.axis_index(axis), x.shape[dim])
+    line, have = (x, 1)
+    while have < ways:
+        line = jnp.concatenate(
+            [line, lax.ppermute(line, axis, [(d, (d - have) % ways) for d in range(ways)])],
+            axis=dim,
+        )
+        have = 2 * have
+    return jnp.roll(line, here * step, axis=dim)
 
 
 def extended_2(block, sides, width):
@@ -48,7 +60,7 @@
         previous, current = (current, following)
     image = apply_blocks(current).astype(jnp.bfloat16)
     factor = 1.0 / (depth * cells * functions)
-    piece = lax.all_gather(current, "band", axis=0, tiled=True)
+    piece = gather_by_bits(current, "band", 0)
     left_part = jnp.einsum("kzsi,czsi->kc", piece, current, preferred_element_type=jnp.float32)
     right_part = jnp.einsum("kzsi,czsi->kc", piece, image, preferred_element_type=jnp.float32)
     partial_terms = jnp.stack([left_part, right_part])

time: 281 us -> 274 us (0.975)
  waiting for transfers between devices: 126 us -> 113 us
  other arithmetic: 5.15 us -> 10.7 us
    all_gather x1 -> x0, waiting for transfers between devices: 17 us -> none  [body(): piece = lax.all_gather(current, 'band', axis=0, tiled=True)]
    reduce_scatter x1, waiting for transfers between devices: 55.9 us -> 60 us  [body(): lax.psum_scatter(partial_terms, 'elem', scatter_dimension=1, tiled=True)]
    concatenate x0 -> x1, other arithmetic: none -> 4.06 us  [gather_by_bits(): return jnp.roll(line, here * step, axis=dim)]
  transfers between devices with their start and end apart: 12 -> 12, of which waited for: 12 -> 11; matrix products, arithmetic and copies ran while one was open for 4% -> 5% of each run, Pallas kernels for 0% -> 0%
where the time goes in v1:
time: 274 us
  waiting for transfers between devices  113 us (41%)
  matrix products  61.3 us (22%)
  local copies, waits for them, and re-layouts  50.1 us (18%)
  starting transfers between devices  24.3 us (9%)
  between operations  14.2 us (5%)
  other arithmetic  10.7 us (4%)
    reduce_scatter x1, waiting for transfers between devices, body(): lax.psum_scatter(partial_terms, 'elem', scatter_dimension=1, tiled=True)  60 us
    dot_general x4, matrix products, apply_blocks(): jnp.einsum('zsdij,czsdj->czsi', hamiltonian, picked, preferred_element_ty...  47.8 us
    gather x5, local copies, waits for them, and re-layouts, apply_blocks(): picked = jnp.take(flat, table, axis=1)  46.8 us
    ppermute x5, waiting for transfers between devices, extended_2(): lax.ppermute(lax.slice_in_dim(block, block.shape[dim] - width, None, axis...  30.4 us
    ppermute x5, waiting for transfers between devices, extended_2(): lax.ppermute(lax.slice_in_dim(block, 0, width, axis=dim), axis, backward)  23 us
    ppermute x5, starting transfers between devices, extended_2(): lax.ppermute(lax.slice_in_dim(block, block.shape[dim] - width, None, axis...  17 us
    dot_general x1, matrix products, body(): jnp.einsum('kzsi,czsi->kc', piece, image, preferred_element_type=jnp.floa...  11.3 us
    ppermute x5, starting transfers between devices, extended_2(): lax.ppermute(lax.slice_in_dim(block, 0, width, axis=dim), axis, backward)  5.73 us
  transfers between devices with their start and end apart: 12, of which 11 were waited for; matrix products, arithmetic and copies ran while one was open for 5% of the time, Pallas kernels for 0%

profile of v1, /device:TPU:0, one launch (start us, length us, event | category | flops | bytes accessed | tf_op | source)
XLA Modules:
  0.0 274.1 jit_solution(14032619705640276675)
XLA Ops:
  8.6 5.5 %collective-permute-start.1 = (bf16[128,1,16,160]{0,3,2,1:T(8,128)(2,1)S(1)}, bf16[128,1,16,160]{0,3,2,1:T(8,128)(2,1)S(1)}, u32[]{:S(2)}, u32[]{:S(2)}) collective-permute-start(bf16[128,1,16,160]{0,3,2,1:T(8,128)(2,1)S(1)} %get-tuple-element.15), channel_id=1, source_target_pairs={{2,0},{4,2},{6,4},{8,6},{10,8},{12,10},{14,12},{16,14},{18,16},{20... | collective-permute-start | bytes 1966088 | tf_op jit(solution)/shard_map/ppermute | solution.py:30
  14.6 7.6 %collective-permute-done.1 = bf16[128,1,16,160]{0,3,2,1:T(8,128)(2,1)S(1)} collective-permute-done((bf16[128,1,16,160]{0,3,2,1:T(8,128)(2,1)S(1)}, bf16[128,1,16,160]{0,3,2,1:T(8,128)(2,1)S(1)}, u32[]{:S(2)}, u32[]{:S(2)}) %collective-permute-start.1) | collective-permute-done | bytes 655392 | tf_op jit(solution)/shard_map/ppermute | solution.py:30
  22.2 4.8 %collective-permute-done = bf16[128,1,16,160]{0,3,2,1:T(8,128)(2,1)} collective-permute-done((bf16[128,1,16,160]{0,3,2,1:T(8,128)(2,1)S(1)}, bf16[128,1,16,160]{0,3,2,1:T(8,128)(2,1)}, u32[]{:S(2)}, u32[]{:S(2)}) %collective-permute-start) | collective-permute-done | bytes 655392 | tf_op jit(solution)/shard_map/ppermute | solution.py:27
  28.8 9.4 %gather_fusion = bf16[224,128,160]{1,2,0:T(8,128)(2,1)} fusion(bf16[128,64,160]{0,2,1:T(8,128)(2,1)S(1)} %bitcast.108, s32[1024]{0:T(1024)S(1)} %pad_clamp_fusion), kind=kCustom, calls=%fused_computation.clone | custom fusion | bytes 18350976 | tf_op jit(solution)/shard_map/jit(_take)/gather | solution.py:49
  38.2 11.3 %fusion.45 = bf16[128,2,16,160]{0,3,2,1:T(8,128)(2,1)S(1)} fusion(bf16[2,16,7,160,160]{4,3,2,1,0:T(8,128)(2,1)} %param.6, bf16[2,16,7,128,160]{3,4,2,1,0:T(8,128)(2,1)} %bitcast.114, pred[2,16,7]{2,1,0:T(8,128)(4,1)S(1)} %copy.14), kind=kOutput, calls=%fused_computation.56 | convolution fusion | flops 1473249280 | bytes 21954784 | tf_op jit(solution)/shard_map/zsdij,czsdj->czsi/dot_general | solution.py:50
  50.2 7.6 %collective-permute-done.3 = bf16[128,1,16,160]{0,3,2,1:T(8,128)(2,1)S(1)} collective-permute-done((bf16[128,1,16,160]{0,3,2,1:T(8,128)(2,1)S(1)}, bf16[128,1,16,160]{0,3,2,1:T(8,128)(2,1)S(1)}, u32[]{:S(2)}, u32[]{:S(2)}) %collective-permute-start.3) | collective-permute-done | bytes 655392 | tf_op jit(solution)/shard_map/ppermute | solution.py:30
  57.8 5.2 %collective-permute-done.2 = bf16[128,1,16,160]{0,3,2,1:T(8,128)(2,1)S(1)} collective-permute-done((bf16[128,1,16,160]{0,3,2,1:T(8,128)(2,1)S(1)}, bf16[128,1,16,160]{0,3,2,1:T(8,128)(2,1)S(1)}, u32[]{:S(2)}, u32[]{:S(2)}) %collective-permute-start.2) | collective-permute-done | bytes 655392 | tf_op jit(solution)/shard_map/ppermute | solution.py:27
  63.3 9.4 %gather_fusion.1 = bf16[224,128,160]{1,2,0:T(8,128)(2,1)} fusion(bf16[128,64,160]{0,2,1:T(8,128)(2,1)S(1)} %bitcast.109, s32[1024]{0:T(1024)S(1)} %pad_clamp_fusion), kind=kCustom, calls=%fused_computation.1.clone | custom fusion | bytes 18350976 | tf_op jit(solution)/shard_map/jit(_take)/gather | solution.py:49
  72.7 11.8 %fusion.28 = bf16[128,2,16,160]{0,3,2,1:T(8,128)(2,1)S(1)} fusion(bf16[128,2,16,160]{0,3,2,1:T(8,128)(2,1)} %param.5, bf16[2,16,7,160,160]{4,3,2,1,0:T(8,128)(2,1)} %param.6, bf16[2,16,7,128,160]{3,4,2,1,0:T(8,128)(2,1)} %bitcast.115, pred[2,16,7]{2,1,0:T(8,128)(4,1)S(1)} %copy.14), kind=kOutput, calls=%fused_computation.49 | convolution fusion | flops 1475215360 | bytes 23265504 | tf_op jit(solution)/shard_map/zsdij,czsdj->czsi/dot_general | solution.py:50
  84.7 4.0 %collective-permute-start.4 = (bf16[128,1,16,160]{0,3,2,1:T(8,128)(2,1)S(1)}, bf16[128,1,16,160]{0,3,2,1:T(8,128)(2,1)S(1)}, u32[]{:S(2)}, u32[]{:S(2)}) collective-permute-start(bf16[128,1,16,160]{0,3,2,1:T(8,128)(2,1)S(1)} %get-tuple-element.10), channel_id=1, source_target_pairs={{0,2},{2,4},{4,6},{6,8},{8,10},{10,12},{12,14},{14,16},{16,18},{18... | collective-permute-start | bytes 1966088 | tf_op jit(solution)/shard_map/ppermute | solution.py:27
  88.6 4.1 %collective-permute-done.5 = bf16[128,1,16,160]{0,3,2,1:T(8,128)(2,1)S(1)} collective-permute-done((bf16[128,1,16,160]{0,3,2,1:T(8,128)(2,1)S(1)}, bf16[128,1,16,160]{0,3,2,1:T(8,128)(2,1)S(1)}, u32[]{:S(2)}, u32[]{:S(2)}) %collective-permute-start.5) | collective-permute-done | bytes 655392 | tf_op jit(solution)/shard_map/ppermute | solution.py:30
  92.8 7.4 %collective-permute-done.4 = bf16[128,1,16,160]{0,3,2,1:T(8,128)(2,1)S(1)} collective-permute-done((bf16[128,1,16,160]{0,3,2,1:T(8,128)(2,1)S(1)}, bf16[128,1,16,160]{0,3,2,1:T(8,128)(2,1)S(1)}, u32[]{:S(2)}, u32[]{:S(2)}) %collective-permute-start.4) | collective-permute-done | bytes 655392 | tf_op jit(solution)/shard_map/ppermute | solution.py:27
  100.4 9.4 %gather_fusion.2 = bf16[224,128,160]{1,2,0:T(8,128)(2,1)} fusion(bf16[128,64,160]{0,2,1:T(8,128)(2,1)S(1)} %bitcast.110, s32[1024]{0:T(1024)S(1)} %pad_clamp_fusion), kind=kCustom, calls=%fused_computation.2.clone | custom fusion | bytes 18350976 | tf_op jit(solution)/shard_map/jit(_take)/gather | solution.py:49
  109.8 11.8 %fusion.27 = bf16[128,2,16,160]{0,3,2,1:T(8,128)(2,1)S(1)} fusion(bf16[128,2,16,160]{0,3,2,1:T(8,128)(2,1)} %copy-done.1, bf16[2,16,7,160,160]{4,3,2,1,0:T(8,128)(2,1)} %param.6, bf16[2,16,7,128,160]{3,4,2,1,0:T(8,128)(2,1)} %bitcast.112, pred[2,16,7]{2,1,0:T(8,128)(4,1)S(1)} %copy.14), kind=kOutput, calls=%fused_computation.46 | convolution fusion | flops 1475215360 | bytes 23265504 | tf_op jit(solution)/shard_map/zsdij,czsdj->czsi/dot_general | solution.py:50
  121.8 5.8 %collective-permute-start.6 = (bf16[128,1,16,160]{0,3,2,1:T(8,128)(2,1)S(1)}, bf16[128,1,16,160]{0,3,2,1:T(8,128)(2,1)S(1)}, u32[]{:S(2)}, u32[]{:S(2)}) collective-permute-start(bf16[128,1,16,160]{0,3,2,1:T(8,128)(2,1)S(1)} %get-tuple-element.8), channel_id=1, source_target_pairs={{0,2},{2,4},{4,6},{6,8},{8,10},{10,12},{12,14},{14,16},{16,18},{18... | collective-permute-start | bytes 1966088 | tf_op jit(solution)/shard_map/ppermute | solution.py:27
  129.9 6.1 %collective-permute-done.6 = bf16[128,1,16,160]{0,3,2,1:T(8,128)(2,1)S(1)} collective-permute-done((bf16[128,1,16,160]{0,3,2,1:T(8,128)(2,1)S(1)}, bf16[128,1,16,160]{0,3,2,1:T(8,128)(2,1)S(1)}, u32[]{:S(2)}, u32[]{:S(2)}) %collective-permute-start.6) | collective-permute-done | bytes 655392 | tf_op jit(solution)/shard_map/ppermute | solution.py:27
  136.3 9.4 %gather_fusion.3 = bf16[224,128,160]{1,2,0:T(8,128)(2,1)} fusion(bf16[128,64,160]{0,2,1:T(8,128)(2,1)S(1)} %bitcast.106, s32[1024]{0:T(1024)S(1)} %pad_clamp_fusion), kind=kCustom, calls=%fused_computation.3.clone | custom fusion | bytes 18350976 | tf_op jit(solution)/shard_map/jit(_take)/gather | solution.py:49
  145.7 12.9 %fusion.26 = bf16[128,2,16,160]{0,3,2,1:T(8,128)(2,1)} fusion(bf16[128,2,16,160]{0,3,2,1:T(8,128)(2,1)} %copy-done, bf16[2,16,7,160,160]{4,3,2,1,0:T(8,128)(2,1)} %param.6, bf16[2,16,7,128,160]{3,4,2,1,0:T(8,128)(2,1)} %bitcast.113, pred[2,16,7]{2,1,0:T(8,128)(4,1)S(1)} %copy.14), kind=kOutput, calls=%fused_computation.43 | convolution fusion | flops 1475215360 | bytes 23265504 | tf_op jit(solution)/shard_map/zsdij,czsdj->czsi/dot_general | solution.py:50
  161.5 6.8 %collective-permute-start.9 = (bf16[128,1,16,160]{0,3,2,1:T(8,128)(2,1)S(1)}, bf16[128,1,16,160]{0,3,2,1:T(8,128)(2,1)}, u32[]{:S(2)}, u32[]{:S(2)}) collective-permute-start(bf16[128,1,16,160]{0,3,2,1:T(8,128)(2,1)S(1)} %get-tuple-element.6), channel_id=1, source_target_pairs={{0,2},{2,4},{4,6},{6,8},{8,10},{10,12},{12,14},{14,16},{16,18},{18... | collective-permute-start | bytes 1966088 | tf_op jit(solution)/shard_map/ppermute | solution.py:27
  169.6 6.9 %collective-permute-done.9 = bf16[128,1,16,160]{0,3,2,1:T(8,128)(2,1)} collective-permute-done((bf16[128,1,16,160]{0,3,2,1:T(8,128)(2,1)S(1)}, bf16[128,1,16,160]{0,3,2,1:T(8,128)(2,1)}, u32[]{:S(2)}, u32[]{:S(2)}) %collective-permute-start.9) | collective-permute-done | bytes 655392 | tf_op jit(solution)/shard_map/ppermute | solution.py:27
  178.2 9.4 %gather_fusion.4 = bf16[224,128,160]{1,2,0:T(8,128)(2,1)} fusion(bf16[128,64,160]{0,2,1:T(8,128)(2,1)S(1)} %bitcast.107, s32[1024]{0:T(1024)S(1)} %pad_clamp_fusion), kind=kCustom, calls=%fused_computation.4.clone | custom fusion | bytes 18350976 | tf_op jit(solution)/shard_map/jit(_take)/gather | solution.py:49
  187.6 4.1 %fusion.25 = bf16[256,2,16,160]{0,3,2,1:T(8,128)(2,1)S(1)} fusion(s32[]{:T(128)S(6)} %select_n.39, bf16[128,2,16,160]{0,3,2,1:T(8,128)(2,1)} %fusion.26, bf16[128,2,16,160]{0,3,2,1:T(8,128)(2,1)} %collective-permute-done.8), kind=kLoop, calls=%fused_computation.35 | loop fusion | flops 10485760 | bytes 5242884 | tf_op jit(solution)/shard_map/jit(_roll_dynamic)/concatenate | solution.py:18
  193.9 11.3 %fusion.63 = f32[1,256,128]{2,1,0:T(8,128)S(1)} fusion(bf16[2,16,7,160,160]{4,3,2,1,0:T(8,128)(2,1)} %param.6, bf16[256,2,16,160]{0,3,2,1:T(8,128)(2,1)S(1)} %fusion.25, bf16[2,16,7,128,160]{3,4,2,1,0:T(8,128)(2,1)} %bitcast.111, pred[2,16,7]{2,1,0:T(8,128)(4,1)S(1)} %copy.14), kind=kOutput, calls=%fused_computation.60 | convolution fusion | flops 1808793600 | bytes 23396576 | tf_op jit(solution)/shard_map/kzsi,czsi->kc/dot_general | solution.py:65
  205.9 60.0 %reduce-scatter.2.cloned.1.call-done = f32[2,16,128]{2,1,0:T(8,128)} async-done(((f32[2,256,128]{2,1,0:T(8,128)}), f32[2,16,128]{2,1,0:T(8,128)}) %reduce-scatter.2.cloned.1.call-update) | async-done | bytes 16400 | tf_op jit(solution)/shard_map/reduce_scatter | solution.py:67
  (39 shorter events, 18.1 us)
Async XLA Ops:
  7.2 7.0 %copy-start.2 = (s32[2,16,6]{1,0,2:T(2,128)S(1)}, s32[2,16,6]{1,0,2:T(2,128)}, u32[]{:S(2)}) copy-start(s32[2,16,6]{1,0,2:T(2,128)} %param.7) | copy-start | bytes 2308
  7.2 258.7 %reduce-scatter.2.cloned.1.call-start = ((), (), s32[]{:S(2)}) async-start(), calls=%async_computation.1 | async-start | bytes 278528 | tf_op jit(solution)/shard_map/reduce_scatter | solution.py:67
  8.6 13.6 %collective-permute-start.1 = (bf16[128,1,16,160]{0,3,2,1:T(8,128)(2,1)S(1)}, bf16[128,1,16,160]{0,3,2,1:T(8,128)(2,1)S(1)}, u32[]{:S(2)}, u32[]{:S(2)}) collective-permute-start(bf16[128,1,16,160]{0,3,2,1:T(8,128)(2,1)S(1)} %get-tuple-element.15), channel_id=1, source_target_pairs={{2,0},{4,2},{6,4},{8,6},{10,8},{12,10},{14,12},{16,14},{18,16},{20... | collective-permute-start | bytes 1966088 | tf_op jit(solution)/shard_map/ppermute | solution.py:30
  14.1 12.9 %collective-permute-start = (bf16[128,1,16,160]{0,3,2,1:T(8,128)(2,1)S(1)}, bf16[128,1,16,160]{0,3,2,1:T(8,128)(2,1)}, u32[]{:S(2)}, u32[]{:S(2)}) collective-permute-start(bf16[128,1,16,160]{0,3,2,1:T(8,128)(2,1)S(1)} %get-tuple-element.14), channel_id=1, source_target_pairs={{0,2},{2,4},{4,6},{6,8},{8,10},{10,12},{12,14},{14,16},{16,18},{18... | collective-permute-start | bytes 1966088 | tf_op jit(solution)/shard_map/ppermute | solution.py:27
  49.5 13.8 %copy-start.1 = (bf16[128,2,16,160]{0,3,2,1:T(8,128)(2,1)}, bf16[128,2,16,160]{0,3,2,1:T(8,128)(2,1)S(1)}, u32[]{:S(2)}) copy-start(bf16[128,2,16,160]{0,3,2,1:T(8,128)(2,1)S(1)} %fusion.45) | copy-start | bytes 3932164
  49.6 8.2 %collective-permute-start.3 = (bf16[128,1,16,160]{0,3,2,1:T(8,128)(2,1)S(1)}, bf16[128,1,16,160]{0,3,2,1:T(8,128)(2,1)S(1)}, u32[]{:S(2)}, u32[]{:S(2)}) collective-permute-start(bf16[128,1,16,160]{0,3,2,1:T(8,128)(2,1)S(1)} %get-tuple-element.13), channel_id=1, source_target_pairs={{2,0},{4,2},{6,4},{8,6},{10,8},{12,10},{14,12},{16,14},{18,16},{20... | collective-permute-start | bytes 1966088 | tf_op jit(solution)/shard_map/ppermute | solution.py:30
  49.7 13.3 %collective-permute-start.2 = (bf16[128,1,16,160]{0,3,2,1:T(8,128)(2,1)S(1)}, bf16[128,1,16,160]{0,3,2,1:T(8,128)(2,1)S(1)}, u32[]{:S(2)}, u32[]{:S(2)}) collective-permute-start(bf16[128,1,16,160]{0,3,2,1:T(8,128)(2,1)S(1)} %get-tuple-element.12), channel_id=1, source_target_pairs={{0,2},{2,4},{4,6},{6,8},{8,10},{10,12},{12,14},{14,16},{16,18},{18... | collective-permute-start | bytes 1966088 | tf_op jit(solution)/shard_map/ppermute | solution.py:27
  84.5 15.9 %copy-start = (bf16[128,2,16,160]{0,3,2,1:T(8,128)(2,1)}, bf16[128,2,16,160]{0,3,2,1:T(8,128)(2,1)S(1)}, u32[]{:S(2)}) copy-start(bf16[128,2,16,160]{0,3,2,1:T(8,128)(2,1)S(1)} %fusion.28) | copy-start | bytes 3932164
  84.6 8.2 %collective-permute-start.5 = (bf16[128,1,16,160]{0,3,2,1:T(8,128)(2,1)S(1)}, bf16[128,1,16,160]{0,3,2,1:T(8,128)(2,1)S(1)}, u32[]{:S(2)}, u32[]{:S(2)}) collective-permute-start(bf16[128,1,16,160]{0,3,2,1:T(8,128)(2,1)S(1)} %get-tuple-element.11), channel_id=1, source_target_pairs={{2,0},{4,2},{6,4},{8,6},{10,8},{12,10},{14,12},{16,14},{18,16},{20... | collective-permute-start | bytes 1966088 | tf_op jit(solution)/shard_map/ppermute | solution.py:30
  84.7 15.4 %collective-permute-start.4 = (bf16[128,1,16,160]{0,3,2,1:T(8,128)(2,1)S(1)}, bf16[128,1,16,160]{0,3,2,1:T(8,128)(2,1)S(1)}, u32[]{:S(2)}, u32[]{:S(2)}) collective-permute-start(bf16[128,1,16,160]{0,3,2,1:T(8,128)(2,1)S(1)} %get-tuple-element.10), channel_id=1, source_target_pairs={{0,2},{2,4},{4,6},{6,8},{8,10},{10,12},{12,14},{14,16},{16,18},{18... | collective-permute-start | bytes 1966088 | tf_op jit(solution)/shard_map/ppermute | solution.py:27
  121.7 8.2 %collective-permute-start.7 = (bf16[128,1,16,160]{0,3,2,1:T(8,128)(2,1)S(1)}, bf16[128,1,16,160]{0,3,2,1:T(8,128)(2,1)S(1)}, u32[]{:S(2)}, u32[]{:S(2)}) collective-permute-start(bf16[128,1,16,160]{0,3,2,1:T(8,128)(2,1)S(1)} %get-tuple-element.9), channel_id=1, source_target_pairs={{2,0},{4,2},{6,4},{8,6},{10,8},{12,10},{14,12},{16,14},{18,16},{20... | collective-permute-start | bytes 1966088 | tf_op jit(solution)/shard_map/ppermute | solution.py:30
  121.8 14.2 %collective-permute-start.6 = (bf16[128,1,16,160]{0,3,2,1:T(8,128)(2,1)S(1)}, bf16[128,1,16,160]{0,3,2,1:T(8,128)(2,1)S(1)}, u32[]{:S(2)}, u32[]{:S(2)}) collective-permute-start(bf16[128,1,16,160]{0,3,2,1:T(8,128)(2,1)S(1)} %get-tuple-element.8), channel_id=1, source_target_pairs={{0,2},{2,4},{4,6},{6,8},{8,10},{10,12},{12,14},{14,16},{16,18},{18... | collective-permute-start | bytes 1966088 | tf_op jit(solution)/shard_map/ppermute | solution.py:27
  158.5 29.1 %collective-permute-start.8 = (bf16[128,2,16,160]{0,3,2,1:T(8,128)(2,1)}, bf16[128,2,16,160]{0,3,2,1:T(8,128)(2,1)}, u32[]{:S(2)}, u32[]{:S(2)}) collective-permute-start(bf16[128,2,16,160]{0,3,2,1:T(8,128)(2,1)} %fusion.26), channel_id=1, source_target_pairs={{0,1},{1,0},{2,3},{3,2},{4,5},{5,4},{6,7},{7,6},{8,9},{9,8},{10,11... | collective-permute-start | bytes 3932168 | tf_op jit(solution)/shard_map/ppermute | solution.py:14
  161.4 8.2 %collective-permute-start.10 = (bf16[128,1,16,160]{0,3,2,1:T(8,128)(2,1)S(1)}, bf16[128,1,16,160]{0,3,2,1:T(8,128)(2,1)S(1)}, u32[]{:S(2)}, u32[]{:S(2)}) collective-permute-start(bf16[128,1,16,160]{0,3,2,1:T(8,128)(2,1)S(1)} %get-tuple-element.7), channel_id=1, source_target_pairs={{2,0},{4,2},{6,4},{8,6},{10,8},{12,10},{14,12},{16,14},{18,16},{20... | collective-permute-start | bytes 1966088 | tf_op jit(solution)/shard_map/ppermute | solution.py:30
  161.5 15.0 %collective-permute-start.9 = (bf16[128,1,16,160]{0,3,2,1:T(8,128)(2,1)S(1)}, bf16[128,1,16,160]{0,3,2,1:T(8,128)(2,1)}, u32[]{:S(2)}, u32[]{:S(2)}) collective-permute-start(bf16[128,1,16,160]{0,3,2,1:T(8,128)(2,1)S(1)} %get-tuple-element.6), channel_id=1, source_target_pairs={{0,2},{2,4},{4,6},{6,8},{8,10},{10,12},{12,14},{14,16},{16,18},{18... | collective-permute-start | bytes 1966088 | tf_op jit(solution)/shard_map/ppermute | solution.py:27
Sparse Core Ops, SparseCore 0:
  206.0 59.8 reduce-scatter.1
